TPU v7x, 256 devices: a whole 4x4x8 slice. The times are simulated.
256 devices in a mesh: dp: 8 (over z_lo, core), expert: 32 (over x, z_hi, y).
Axes of the slice: x: 4, y: 4, z: 8 (z_hi: 2, z_lo: 4; z = z_hi * 4 + z_lo), core: 2. Of those that a mesh axis runs over, the one named last changes fastest.
Arguments:
- tokens: bfloat16 [16384, 2048], P(('dp', 'expert')), may hold values from -6 to 6
- routes: int32 [16384, 8], P(('dp', 'expert')), may hold values from 0 to 63, all different within a row; in each aligned block of 64 rows (0 to 63, 64 to 127, ...) at most 12 rows name the same one
- route_weight: int32 [16384, 8], P(('dp', 'expert')), may hold values from 1 to 65535
- capacity: int32 [64], replicated, may hold values from 8 to 10
- hot_expert: int32 [1], replicated, may hold values from 0 to 63
- w_gate: bfloat16 [64, 2048, 768], P('expert', 'dp'), may hold values from -0.125 to 0.125
- w_up: bfloat16 [64, 2048, 768], P('expert', 'dp'), may hold values from -0.125 to 0.125
- w_down: bfloat16 [64, 768, 2048], P('expert', None, 'dp'), may hold values from -0.21875 to 0.21875
Outputs:
- mixed: bfloat16 [16384, 2048], P(('dp', 'expert'))
All inputs are finite; a program needn't handle non-finite values.
Results may differ from a plain program's by a relative error of at most 0.0057.
Values may be sent and summed in bfloat16 or wider, within the bound.
No kernel may reach another device: no remote copies, remote signals or barrier semaphores. Data moves between devices by JAX's collectives and lax.ppermute only.
A program may use at most 128 MiB of HBM per device.

v0:
```python
import jax
import jax.numpy as jnp
from jax import lax
from jax.sharding import PartitionSpec as P

CAP = 10
MOST = 12


def per_device(tokens, routes, route_weight, capacity, hot_expert, w_gate, w_up, w_down):
    tok_rows = tokens.shape[0]
    width = tokens.shape[1]
    n_peer = lax.axis_size("expert")
    my_index = lax.axis_index("expert")
    exp_dev = w_gate.shape[0]
    experts = exp_dev * n_peer
    flat_e = routes.reshape(-1)
    weights = route_weight.astype(jnp.float32)
    share = (weights / jnp.sum(weights, axis=1, keepdims=True)).reshape(-1)
    onehot = (flat_e[:, None] == jnp.arange(experts, dtype=jnp.int32)[None, :]).astype(jnp.int32)
    before = jnp.cumsum(onehot, axis=0) - onehot
    rank = jnp.sum(onehot * before, axis=1)
    cap_of = jnp.sum(onehot * capacity[None, :], axis=1)
    hot = hot_expert[0]
    owner = hot // exp_dev
    hot_local = jnp.clip(hot - my_index * exp_dev, 0, exp_dev - 1)
    is_hot = flat_e == hot
    kept_cap = jnp.logical_and(jnp.logical_not(is_hot), rank < cap_of)
    target_cap = jnp.where(kept_cap, flat_e * CAP + rank, -1).reshape(tok_rows, -1)
    target_hot = jnp.where(is_hot, rank, -1).reshape(tok_rows, -1)
    select_cap = jnp.any(
        target_cap[None, :, :] == jnp.arange(experts * CAP, dtype=jnp.int32)[:, None, None], axis=2
    ).astype(jnp.bfloat16)
    select_hot = jnp.any(
        target_hot[None, :, :] == jnp.arange(MOST, dtype=jnp.int32)[:, None, None], axis=2
    ).astype(jnp.bfloat16)
    send_cap = jnp.dot(select_cap, tokens, preferred_element_type=jnp.float32).astype(jnp.bfloat16)
    send_cap = send_cap.reshape(n_peer, exp_dev * CAP, width)
    hot_rows = jnp.dot(select_hot, tokens, preferred_element_type=jnp.float32).astype(jnp.bfloat16)
    cap_slots = exp_dev * CAP
    owner_mask = (jnp.arange(n_peer, dtype=jnp.int32) == owner)[:, None, None]
    send_hot = jnp.where(owner_mask, hot_rows[None, :, :], jnp.zeros((), jnp.bfloat16))
    received = lax.all_to_all(
        jnp.concatenate([send_cap, send_hot], axis=1),
        "expert",
        split_axis=0,
        concat_axis=0,
        tiled=True,
    )
    recv_cap = received[:, :cap_slots].reshape(n_peer, exp_dev, CAP, width)
    recv_hot = received[:, cap_slots:]
    piece_gate = lax.all_gather(w_gate, "dp", axis=1, tiled=True)
    piece_up = lax.all_gather(w_up, "dp", axis=1, tiled=True)
    hot_gate = lax.dynamic_index_in_dim(piece_gate, hot_local, 0, keepdims=False)
    hot_up = lax.dynamic_index_in_dim(piece_up, hot_local, 0, keepdims=False)
    gate_cap = jnp.einsum(
        "pcrd,cdf->pcrf", recv_cap, piece_gate, preferred_element_type=jnp.float32
    )
    up_cap = jnp.einsum("pcrd,cdf->pcrf", recv_cap, piece_up, preferred_element_type=jnp.float32)
    gate_hot = jnp.einsum("prd,df->prf", recv_hot, hot_gate, preferred_element_type=jnp.float32)
    up_hot = jnp.einsum("prd,df->prf", recv_hot, hot_up, preferred_element_type=jnp.float32)
    gate_cap, up_cap, gate_hot, up_hot = (gate_cap, up_cap, gate_hot, up_hot)
    hidden_cap = (jax.nn.silu(gate_cap) * up_cap).astype(jnp.bfloat16)
    hidden_hot = (jax.nn.silu(gate_hot) * up_hot).astype(jnp.bfloat16)
    piece = lax.all_gather(w_down, "dp", axis=2, tiled=True)
    count = piece.shape[2]
    hot_down = lax.dynamic_index_in_dim(piece, hot_local, 0, keepdims=False)
    out_cap = jnp.einsum("pcrf,cfd->pcrd", hidden_cap, piece, preferred_element_type=jnp.float32)
    out_hot = jnp.einsum("prf,fd->prd", hidden_hot, hot_down, preferred_element_type=jnp.float32)
    out_cap = out_cap.reshape(n_peer, cap_slots, count)
    outgoing = jnp.concatenate([out_cap, out_hot], axis=1).astype(jnp.bfloat16)
    returned = lax.all_to_all(outgoing, "expert", split_axis=0, concat_axis=0, tiled=True)
    back_cap = returned[:, :cap_slots].reshape(experts * CAP, width)
    back_hot = lax.dynamic_index_in_dim(returned, owner, 0, keepdims=False)[cap_slots:]
    table = jnp.concatenate([back_cap, back_hot, jnp.zeros((1, width), jnp.bfloat16)], axis=0)
    where_row = jnp.where(
        kept_cap, flat_e * CAP + rank, jnp.where(is_hot, experts * CAP + rank, experts * CAP + MOST)
    )
    picked = jnp.take(table, where_row, axis=0)
    factor = jnp.where(jnp.logical_or(kept_cap, is_hot), share, 0.0)
    summed = jnp.sum(
        (picked.astype(jnp.float32) * factor[:, None]).reshape(tok_rows, -1, width), axis=1
    )
    return summed.astype(jnp.bfloat16)


def solution(mesh):
    in_specs = (
        P(("dp", "expert"), None),
        P(("dp", "expert"), None),
        P(("dp", "expert"), None),
        P(),
        P(),
        P("expert", "dp", None),
        P("expert", "dp", None),
        P("expert", None, "dp"),
    )
    out_specs = P(("dp", "expert"), None)
    return jax.shard_map(
        per_device, mesh=mesh, in_specs=in_specs, out_specs=out_specs, check_vma=False
    )
```

profile of v0, /device:TPU:37, one launch (start us, length us, event | category | flops | bytes accessed | tf_op | source)
XLA Modules:
  0.0 495.2 jit_solution(10126614187241409905)
XLA Ops:
  6.5 0.0 copy-start
  6.5 0.0 copy-start.4
  6.5 0.0 all-gather.4.cloned.1.call-start
  6.5 0.7 all-gather.4.cloned.1.call-update
  7.3 0.0 all-gather.6.cloned.1.call-start
  7.3 0.7 all-gather.6.cloned.1.call-update
  8.0 0.0 all-gather.8.cloned.1.call-start
  8.1 0.7 all-gather.8.cloned.1.call-update
  9.4 0.8 copy.35
  10.2 0.1 eq.89
  10.3 0.1 reshape.156
  10.4 1.2 reduce-window.6
  11.6 0.2 slice_reduce_fusion
  11.9 0.0 copy-done.4
  11.9 0.1 select_reduce_fusion
  12.0 0.1 reduce_sum.45
  12.1 0.1 reduce_sum.47
  12.3 0.1 copy.40
  12.3 0.5 fusion.35
  12.8 0.0 copy-done
  12.8 2.4 convolution_convert_fusion
  15.2 3.5 reshape.158
  18.8 0.1 convolution_convert_fusion.1
  18.9 0.2 broadcast_select_fusion
  19.1 2.7 pad_maximum_fusion
  21.8 13.0 %all-to-all-start = ((bf16[32,32,2048]{2,1,0:T(8,128)(2,1)}), bf16[32,32,2048]{2,1,0:T(8,128)(2,1)}, u32[]{:S(2)}, u32[]{:S(2)}) async-start(bf16[32,32,2048]{2,1,0:T(8,128)(2,1)} %pad_maximum_fusion), calls=%async_computation | async-start | bytes 8388608 | tf_op jit(solution)/shard_map/all_to_all | solution.py:43
  34.9 139.3 %all-to-all-done = bf16[32,32,2048]{2,1,0:T(8,128)(2,1)} async-done(((bf16[32,32,2048]{2,1,0:T(8,128)(2,1)}), bf16[32,32,2048]{2,1,0:T(8,128)(2,1)}, u32[]{:S(2)}, u32[]{:S(2)}) %all-to-all-start) | async-done | bytes 4194336 | tf_op jit(solution)/shard_map/all_to_all | solution.py:43
  174.1 2.3 slice.31
  176.5 1.4 copy.41
  177.9 3.6 slice.32
  181.5 0.0 all-gather.4.cloned.1.call-done
  181.5 6.3 %fusion.4 = f32[2,32,10,768]{3,1,2,0:T(8,128)} fusion(bf16[32,2,10,2048]{3,0,2,1:T(8,128)(2,1)S(1)} %bitcast.108, bf16[2,2048,768]{2,1,0:T(8,128)(2,1)} %all-gather.4.cloned.1.call-done), kind=kOutput, calls=%fused_computation.5 | convolution fusion | flops 2013265920 | bytes 10878976 | tf_op jit(solution)/shard_map/pcrd,cdf->pcrf/dot_general | solution.py:56
  187.9 61.1 %all-gather.6.cloned.1.call-done = bf16[2,2048,768]{2,1,0:T(8,128)(2,1)} async-done(((bf16[2,256,768]{2,1,0:T(8,128)(2,1)}), bf16[2,2048,768]{2,1,0:T(8,128)(2,1)}) %all-gather.6.cloned.1.call-update) | async-done | bytes 6291472 | tf_op jit(solution)/shard_map/all_gather | solution.py:53
  248.9 75.1 %all-gather.8.cloned.1.call-done = bf16[2,768,2048]{2,1,0:T(8,128)(2,1)} async-done(((bf16[2,768,256]{2,1,0:T(8,128)(2,1)}), bf16[2,768,2048]{2,1,0:T(8,128)(2,1)}) %all-gather.8.cloned.1.call-update) | async-done | bytes 6291472 | tf_op jit(solution)/shard_map/all_gather | solution.py:65
  324.0 11.0 %fusion.6 = bf16[2,32,10,2048]{3,1,2,0:T(8,128)(2,1)} fusion(bf16[2,768,2048]{2,1,0:T(8,128)(2,1)} %all-gather.8.cloned.1.call-done, f32[2,32,10,768]{3,1,2,0:T(8,128)} %fusion.4, bf16[32,2,10,2048]{3,0,2,1:T(8,128)(2,1)S(1)} %bitcast.109, bf16[2,2048,768]{2,1,0:T(8,128)(2,1)} %all-gather.6.cloned.1.call-done), kind=kOutput, calls=%fused_computation.10 | convolution fusion | flops 4030791680 | bytes 19791872 | tf_op jit(solution)/shard_map/pcrf,cfd->pcrd/dot_general | solution.py:68
  334.9 0.0 copy-start.2
  334.9 3.3 copy.43
  338.3 0.0 copy-done.2
  338.3 5.2 %fusion.13 = f32[32,12,768]{2,0,1:T(8,128)} fusion(bf16[2,2048,768]{2,1,0:T(8,128)(2,1)} %all-gather.4.cloned.1.call-done, s32[]{:T(128)S(6)} %min.4, bf16[32,12,2048]{2,1,0:T(8,128)(2,1)S(1)} %copy-done.2), kind=kOutput, calls=%fused_computation.16 | convolution fusion | flops 1207959552 | bytes 5898244 | tf_op jit(solution)/shard_map/prd,df->prf/dot_general | solution.py:60
  343.5 8.7 %fusion.18 = bf16[32,12,2048]{2,0,1:T(8,128)(2,1)} fusion(bf16[2,768,2048]{2,1,0:T(8,128)(2,1)} %all-gather.8.cloned.1.call-done, s32[]{:T(128)S(6)} %min.4, bf16[2,2048,768]{2,1,0:T(8,128)(2,1)} %all-gather.6.cloned.1.call-done, f32[32,12,768]{2,0,1:T(8,128)} %fusion.13, bf16[32,12,2048]{2,1,0:T(8,128)(2,1)} %slice.32), kind=kOutput, calls=%fused_computation.21 | convolution fusion | flops 2418475008 | bytes 11142144 | tf_op jit(solution)/shard_map/prf,fd->prd/dot_general | solution.py:69
  352.2 2.3 copy.44
  354.5 2.6 pad_maximum_fusion.1
  357.1 0.0 copy-start.3
  357.1 9.8 %all-to-all-start.1 = ((bf16[32,32,2048]{2,1,0:T(8,128)(2,1)}), bf16[32,32,2048]{2,1,0:T(8,128)(2,1)}, u32[]{:S(2)}, u32[]{:S(2)}) async-start(bf16[32,32,2048]{2,1,0:T(8,128)(2,1)} %pad_maximum_fusion.1), calls=%async_computation.1 | async-start | bytes 8388608 | tf_op jit(solution)/shard_map/all_to_all | solution.py:72
  367.0 0.1 eq.101
  367.1 0.0 copy-done.3
  367.1 0.1 copy.45
  367.2 0.1 mul.65
  367.2 0.1 pad.2.clone
  367.3 0.1 convert_reduce_fusion
  367.5 0.1 divide_select_fusion
  367.6 105.7 %all-to-all-done.1 = bf16[32,32,2048]{2,1,0:T(8,128)(2,1)} async-done(((bf16[32,32,2048]{2,1,0:T(8,128)(2,1)}), bf16[32,32,2048]{2,1,0:T(8,128)(2,1)}, u32[]{:S(2)}, u32[]{:S(2)}) %all-to-all-start.1) | async-done | bytes 4194336 | tf_op jit(solution)/shard_map/all_to_all | solution.py:72
  473.3 2.1 slice.33
  475.4 2.2 reshape.161
  477.7 0.9 dynamic-slice_bitcast_fusion
  478.5 2.2 maximum_maximum_fusion
  480.8 0.0 copy-start.1
  480.8 3.3 gather_fusion
  484.1 4.5 multiply_reduce_fusion
  488.7 0.0 copy-done.1
  (9 shorter events, 0.2 us)
Async XLA Ops:
  6.5 6.3 %copy-start = (bf16[64,2048]{1,0:T(8,128)(2,1)S(1)}, bf16[64,2048]{1,0:T(8,128)(2,1)}, u32[]{:S(2)}) copy-start(bf16[64,2048]{1,0:T(8,128)(2,1)} %param.8) | copy-start | bytes 786436
  6.5 5.3 %copy-start.4 = (s32[64]{0:T(128)S(1)}, s32[64]{0:T(128)}, u32[]{:S(2)}) copy-start(s32[64]{0:T(128)} %param.11) | copy-start | bytes 772
  6.5 175.0 %all-gather.4.cloned.1.call-start = ((), (), s32[]{:S(2)}) async-start(), calls=%async_computation.2 | async-start | bytes 7077888 | tf_op jit(solution)/shard_map/all_gather | solution.py:52
  7.3 241.6 %all-gather.6.cloned.1.call-start = ((), (), s32[]{:S(2)}) async-start(), calls=%async_computation.3 | async-start | bytes 7077888 | tf_op jit(solution)/shard_map/all_gather | solution.py:53
  8.0 315.9 %all-gather.8.cloned.1.call-start = ((), (), s32[]{:S(2)}) async-start(), calls=%async_computation.4 | async-start | bytes 7077888 | tf_op jit(solution)/shard_map/all_gather | solution.py:65
  21.8 152.3 %all-to-all-start = ((bf16[32,32,2048]{2,1,0:T(8,128)(2,1)}), bf16[32,32,2048]{2,1,0:T(8,128)(2,1)}, u32[]{:S(2)}, u32[]{:S(2)}) async-start(bf16[32,32,2048]{2,1,0:T(8,128)(2,1)} %pad_maximum_fusion), calls=%async_computation | async-start | bytes 8388608 | tf_op jit(solution)/shard_map/all_to_all | solution.py:43
  334.9 3.4 copy-start.2
  357.1 10.0 %copy-start.3 = (s32[64,8]{0,1:T(8,128)S(1)}, s32[64,8]{0,1:T(8,128)}, u32[]{:S(2)}) copy-start(s32[64,8]{0,1:T(8,128)} %param.10) | copy-start | bytes 6148
  357.1 116.2 %all-to-all-start.1 = ((bf16[32,32,2048]{2,1,0:T(8,128)(2,1)}), bf16[32,32,2048]{2,1,0:T(8,128)(2,1)}, u32[]{:S(2)}, u32[]{:S(2)}) async-start(bf16[32,32,2048]{2,1,0:T(8,128)(2,1)} %pad_maximum_fusion.1), calls=%async_computation.1 | async-start | bytes 8388608 | tf_op jit(solution)/shard_map/all_to_all | solution.py:72
  480.8 7.9 %copy-start.1 = (bf16[64,2048]{1,0:T(8,128)(2,1)S(1)}, bf16[64,2048]{1,0:T(8,128)(2,1)}, u32[]{:S(2)}) copy-start(bf16[64,2048]{1,0:T(8,128)(2,1)} %param.8) | copy-start | bytes 786436
Sparse Core Ops, SparseCore 0:
  9.1 164.8 all-gather.3
  175.8 73.0 all-gather.5
  250.6 73.2 all-gather.7
where the time goes:
time: 496 us; the launch traced here: 495 us
  waiting for transfers between devices  383 us (77%)
  matrix products  33.7 us (7%)
  local copies, waits for them, and re-layouts  26.9 us (5%)
  starting transfers between devices  23 us (5%)
  other arithmetic  14.4 us (3%)
  between operations  14 us (3%)
    all_to_all x1, waiting for transfers between devices, per_device(): lax.all_to_all(jnp.concatenate([send_cap, send_hot], axis=1), 'expert', s...  139 us
    all_to_all x1, waiting for transfers between devices, per_device(): lax.all_to_all(outgoing, 'expert', split_axis=0, concat_axis=0, tiled=True)  106 us
    all_gather x1, waiting for transfers between devices, per_device(): piece = lax.all_gather(w_down, 'dp', axis=2, tiled=True)  75.1 us
    all_gather x1, waiting for transfers between devices, per_device(): piece_up = lax.all_gather(w_up, 'dp', axis=1, tiled=True)  61.1 us
    all_to_all x1, starting transfers between devices, per_device(): lax.all_to_all(jnp.concatenate([send_cap, send_hot], axis=1), 'expert', s...  13 us
    dot_general x1, matrix products, per_device(): jnp.einsum('pcrf,cfd->pcrd', hidden_cap, piece, preferred_element_type=jn...  11 us
  transfers between devices with their start and end apart: 5, of which 4 were waited for; matrix products, arithmetic and copies ran while one was open for 5% of the time, Pallas kernels for 0%

commit v1 on v0

--- a/solution.py
+++ b/solution.py
@@ -50,7 +50,9 @@
     recv_cap = received[:, :cap_slots].reshape(n_peer, exp_dev, CAP, width)
     recv_hot = received[:, cap_slots:]
     piece_gate = lax.all_gather(w_gate, "dp", axis=1, tiled=True)
-    piece_up = lax.all_gather(w_up, "dp", axis=1, tiled=True)
+    piece_up = jnp.concatenate(
+        lax.all_to_all(jnp.stack([w_up] * lax.axis_size("dp")), "dp", 0, 0), axis=1
+    )
     hot_gate = lax.dynamic_index_in_dim(piece_gate, hot_local, 0, keepdims=False)
     hot_up = lax.dynamic_index_in_dim(piece_up, hot_local, 0, keepdims=False)
     gate_cap = jnp.einsum(

time: 496 us -> 556 us (1.12)
  the two profiles are of different devices: /device:TPU:37 before, /device:TPU:64 now
where the time goes in v1:
time: 556 us; the launch traced here: 555 us
  waiting for transfers between devices  291 us (52%)
  blocking collectives  157 us (28%)
  local copies, waits for them, and re-layouts  34.2 us (6%)
  matrix products  34 us (6%)
  between operations  14.3 us (3%)
  other arithmetic  14 us (3%)
  starting transfers between devices  10.3 us (2%)
    all_to_all x1, waiting for transfers between devices, per_device(): lax.all_to_all(jnp.stack([w_up] * lax.axis_size('dp')), 'dp', 0, 0)  188 us
    all_to_all x1, blocking collectives, per_device(): lax.all_to_all(jnp.concatenate([send_cap, send_hot], axis=1), 'expert', s...  157 us
    all_to_all x1, waiting for transfers between devices, per_device(): lax.all_to_all(outgoing, 'expert', split_axis=0, concat_axis=0, tiled=True)  101 us
    dot_general x1, matrix products, per_device(): jnp.einsum('pcrf,cfd->pcrd', hidden_cap, piece, preferred_element_type=jn...  12 us
  transfers between devices with their start and end apart: 4, of which 2 were waited for; matrix products, arithmetic and copies ran while one was open for 5% of the time, Pallas kernels for 0%

profile of v1, /device:TPU:64, one launch (start us, length us, event | category | flops | bytes accessed | tf_op | source)
XLA Modules:
  0.0 554.9 jit_solution(11819927315363037683)
XLA Ops:
  6.5 0.0 copy-start
  6.5 0.0 all-gather.3.cloned.1.call-start
  6.5 0.7 all-gather.3.cloned.1.call-update
  7.3 0.8 copy.36
  8.0 0.1 eq.89
  8.8 0.1 reshape.164
  8.9 1.2 reduce-window.6
  10.1 0.2 slice_reduce_fusion
  10.4 0.8 select_reduce_fusion
  11.2 0.1 reduce_sum.45
  11.3 0.1 reduce_sum.47
  11.4 0.1 copy.41
  11.5 0.5 fusion.29
  12.0 0.0 copy-done
  12.0 2.4 convolution_convert_fusion
  14.4 3.5 reshape.166
  18.0 0.1 convolution_convert_fusion.1
  18.2 0.2 broadcast_select_fusion
  18.4 1.5 pad_maximum_fusion
  19.8 0.0 copy-start.4
  19.9 157.2 %all_to_all.15 = bf16[32,32,2048]{2,1,0:T(8,128)(2,1)} all-to-all(bf16[32,32,2048]{2,1,0:T(8,128)(2,1)S(1)} %pad_maximum_fusion), channel_id=1, replica_groups=mesh['dp'=8,'expert'=32] {'expert'}, dimensions={0} | all-to-all | bytes 8388608 | tf_op jit(solution)/shard_map/all_to_all | solution.py:43
  177.0 0.0 copy-done.4
  177.0 3.2 stack.2
  180.3 5.3 all-to-all-start.1
  185.5 0.0 all-gather.5.cloned.1.call-start
  185.5 0.7 all-gather.5.cloned.1.call-update
  186.3 0.0 slice-start
  186.3 1.9 slice-done
  188.2 0.0 copy-start.2
  188.2 2.9 copy.42
  191.1 0.0 copy-done.2
  191.1 0.7 slice.32
  191.8 188.4 %all-to-all-done.1 = bf16[8,2,256,768]{3,2,1,0:T(8,128)(2,1)} async-done(((bf16[8,2,256,768]{3,2,1,0:T(8,128)(2,1)}), bf16[8,2,256,768]{3,2,1,0:T(8,128)(2,1)}, u32[]{:S(2)}, u32[]{:S(2)}) %all-to-all-start.1) | async-done | bytes 6291488 | tf_op jit(solution)/shard_map/all_to_all | solution.py:54
  380.2 6.0 %copy.43 = bf16[8,2,256,768]{3,2,0,1:T(8,128)(2,1)} copy(bf16[8,2,256,768]{3,2,1,0:T(8,128)(2,1)} %all-to-all-done.1) | data formatting | bytes 12582912 | tf_op jit(solution)/shard_map/all_to_all | solution.py:54
  386.1 0.0 all-gather.3.cloned.1.call-done
  386.1 5.2 fusion.11
  391.3 0.0 all-gather.5.cloned.1.call-done
  391.3 7.9 %fusion.16 = bf16[32,12,2048]{2,0,1:T(8,128)(2,1)} fusion(bf16[2,768,2048]{2,1,0:T(8,128)(2,1)} %all-gather.5.cloned.1.call-done, s32[]{:T(128)S(6)} %min.4, bf16[2,2048,768]{2,1,0:T(8,128)(2,1)} %bitcast.107, f32[32,12,768]{2,0,1:T(8,128)} %fusion.11, bf16[32,12,2048]{2,1,0:T(8,128)(2,1)S(1)} %slice.32), kind=kOutput, calls=%fused_computation.19 | convolution fusion | flops 2418475008 | bytes 10617856 | tf_op jit(solution)/shard_map/prf,fd->prd/dot_general | solution.py:71
  399.2 0.0 copy-start.3
  399.2 2.4 copy.46
  401.7 0.0 copy-done.3
  401.7 6.3 %fusion.2 = f32[2,32,10,768]{3,1,2,0:T(8,128)} fusion(bf16[32,2,10,2048]{3,0,2,1:T(8,128)(2,1)S(1)} %bitcast.110, bf16[2,2048,768]{2,1,0:T(8,128)(2,1)} %all-gather.3.cloned.1.call-done), kind=kOutput, calls=%fused_computation.3 | convolution fusion | flops 2013265920 | bytes 10878976 | tf_op jit(solution)/shard_map/pcrd,cdf->pcrf/dot_general | solution.py:58
  408.0 12.0 %fusion.4 = bf16[2,32,10,2048]{3,1,2,0:T(8,128)(2,1)} fusion(bf16[2,768,2048]{2,1,0:T(8,128)(2,1)} %all-gather.5.cloned.1.call-done, f32[2,32,10,768]{3,1,2,0:T(8,128)} %fusion.2, bf16[32,2,10,2048]{3,0,2,1:T(8,128)(2,1)} %bitcast.109, bf16[2,2048,768,1]{2,1,3,0:T(8,128)(2,1)} %bitcast.108), kind=kOutput, calls=%fused_computation.8 | convolution fusion | flops 4030791680 | bytes 19791872 | tf_op jit(solution)/shard_map/pcrf,cfd->pcrd/dot_general | solution.py:70
  420.0 3.2 copy.45
  423.2 2.7 pad_maximum_fusion.1
  425.9 0.0 copy-start.5
  425.9 5.0 all-to-all-start.2
  430.9 0.1 eq.101
  431.0 0.0 copy-done.5
  431.0 0.1 copy.47
  431.1 0.1 mul.65
  431.1 0.1 pad.2.clone
  431.3 0.1 convert_reduce_fusion
  431.4 0.1 divide_select_fusion
  431.5 101.2 %all-to-all-done.2 = bf16[32,32,2048]{2,1,0:T(8,128)(2,1)} async-done(((bf16[32,32,2048]{2,1,0:T(8,128)(2,1)}), bf16[32,32,2048]{2,1,0:T(8,128)(2,1)}, u32[]{:S(2)}, u32[]{:S(2)}) %all-to-all-start.2) | async-done | bytes 4194336 | tf_op jit(solution)/shard_map/all_to_all | solution.py:74
  532.7 2.1 slice.33
  534.8 2.2 reshape.171
  537.1 0.9 dynamic-slice_bitcast_fusion
  537.9 2.2 maximum_maximum_fusion
  540.2 0.0 copy-start.1
  540.2 3.3 gather_fusion
  543.5 4.5 multiply_reduce_fusion
  548.1 0.0 copy-done.1
  (9 shorter events, 0.2 us)
Async XLA Ops:
  6.5 5.4 copy-start
  6.5 379.6 %all-gather.3.cloned.1.call-start = ((), (), s32[]{:S(2)}) async-start(), calls=%async_computation.3 | async-start | bytes 7077888 | tf_op jit(solution)/shard_map/all_gather | solution.py:52
  19.8 157.2 %copy-start.4 = (bf16[2,256,768]{2,1,0:T(8,128)(2,1)S(1)}, bf16[2,256,768]{2,1,0:T(8,128)(2,1)}, u32[]{:S(2)}) copy-start(bf16[2,256,768]{2,1,0:T(8,128)(2,1)} %param.14) | copy-start | bytes 2359300
  180.3 199.9 %all-to-all-start.1 = ((bf16[8,2,256,768]{3,2,1,0:T(8,128)(2,1)}), bf16[8,2,256,768]{3,2,1,0:T(8,128)(2,1)}, u32[]{:S(2)}, u32[]{:S(2)}) async-start(bf16[8,2,256,768]{3,2,1,0:T(8,128)(2,1)} %stack.2), calls=%async_computation.1 | async-start | bytes 12582912 | tf_op jit(solution)/shard_map/all_to_all | solution.py:54
  185.5 205.8 %all-gather.5.cloned.1.call-start = ((), (), s32[]{:S(2)}) async-start(), calls=%async_computation.4 | async-start | bytes 7077888 | tf_op jit(solution)/shard_map/all_gather | solution.py:67
  186.3 1.9 slice-start
  188.2 2.9 copy-start.2
  399.2 2.5 copy-start.3
  425.9 5.1 copy-start.5
  425.9 106.8 %all-to-all-start.2 = ((bf16[32,32,2048]{2,1,0:T(8,128)(2,1)}), bf16[32,32,2048]{2,1,0:T(8,128)(2,1)}, u32[]{:S(2)}, u32[]{:S(2)}) async-start(bf16[32,32,2048]{2,1,0:T(8,128)(2,1)} %pad_maximum_fusion.1), calls=%async_computation.2 | async-start | bytes 8388608 | tf_op jit(solution)/shard_map/all_to_all | solution.py:74
  540.2 7.9 %copy-start.1 = (bf16[64,2048]{1,0:T(8,128)(2,1)S(1)}, bf16[64,2048]{1,0:T(8,128)(2,1)}, u32[]{:S(2)}) copy-start(bf16[64,2048]{1,0:T(8,128)(2,1)} %param.8) | copy-start | bytes 786436
Sparse Core Ops, SparseCore 0:
  9.1 162.8 all-gather.2
  188.1 191.8 all-gather.4
